TPU v7x, 256 devices: a whole 4x4x8 slice. The times are simulated.
256 devices in a mesh: seq: 32 (over x, y, core), head: 8 (over z).
Axes of the slice: x: 4, y: 4, z: 8, core: 2. Of those that a mesh axis runs over, the one named last changes fastest.
Arguments:
- queries: float32 [16384, 1024], P('seq', 'head'), may hold values from -6 to 6
- keys: float32 [16384, 1024], P('seq', 'head'), may hold values from -5 to 5
- values: float32 [16384, 1024], P('seq', 'head'), may hold values from -15 to 15
- gain: float32 [1024], P('head'), may hold values from 0.1 to 1.9
- ridge: float32 [8], P('head'), may hold values from 0.01 to 0.1
- prior_gram: float32 [8, 128, 128], P('head'), as said below
- prior_cross: float32 [8, 128, 128], P('head')
- cotangent: float32 [16384, 1024], P('seq', 'head'), may hold values from -6 to 6
Outputs:
- normed: float32 [16384, 1024], P('seq', 'head')
- grad_queries: float32 [16384, 1024], P('seq', 'head')
- grad_keys: float32 [16384, 1024], P('seq', 'head')
- grad_values: float32 [16384, 1024], P('seq', 'head')
Inputs may be any that keep to these rules, and one draw needn't show every extreme that they name: `prior_gram`: each head's matrix is symmetric positive definite.
All inputs are finite; a program needn't handle non-finite values.
Results may differ from a plain program's by a relative error of at most 0.0003.
Values sent between devices are 32-bit elements; how exact they have to be, the bound alone decides.
A program may use at most 64 MiB of HBM per device.

v0:
```python
import jax
import jax.numpy as jnp
from jax import lax
from jax.sharding import PartitionSpec as P

DH = 128
ITERS = 8
epsilon = 1e-06


def prefix(part, axis, combine, identity, reverse):
    count = lax.axis_size(axis)
    place = lax.axis_index(axis)
    ahead = count - 1 - place if reverse else place
    gathered = jax.tree.map(lambda a: lax.all_gather(a, axis), part)
    state = jax.tree.map(lambda a, e: jnp.zeros_like(a) + jnp.asarray(e, a.dtype), part, identity)

    def one(turn, state):
        source = count - 1 - turn if reverse else turn
        return combine(
            state, jax.tree.map(lambda a: lax.dynamic_index_in_dim(a, source, 0, False), gathered)
        )

    return lax.fori_loop(0, ahead, one, state)


def block_forward(query, keyset, valueset, start_gram, start_cross, ridge_value, first_row):
    highest = lax.Precision.HIGHEST
    count = query.shape[0]
    places = jnp.arange(count)
    causal = (places[None, :] <= places[:, None]).astype(jnp.float32)
    damping = ridge_value * (first_row + places + 1).astype(jnp.float32)[:, None]

    def apply_system(search):
        inner = jnp.dot(search, keyset.T, precision=highest) * causal
        return (
            jnp.dot(search, start_gram, precision=highest)
            + jnp.dot(inner, keyset, precision=highest)
            + damping * search
        )

    def cg_step(carry, unused):
        solution, residual, search, squared = carry
        image = apply_system(search)
        alpha = squared / jnp.sum(search * image, axis=1, keepdims=True)
        solution = solution + alpha * search
        residual = residual - alpha * image
        squared_next = jnp.sum(residual * residual, axis=1, keepdims=True)
        search = residual + squared_next / squared * search
        return ((solution, residual, search, squared_next), None)

    squared = jnp.sum(query * query, axis=1, keepdims=True)
    start = (jnp.zeros_like(query), query, query, squared)
    (solution, _, _, _), _ = lax.scan(cg_step, start, None, length=ITERS)
    inner = jnp.dot(solution, keyset.T, precision=highest) * causal
    return jnp.dot(solution, start_cross, precision=highest) + jnp.dot(
        inner, valueset, precision=highest
    )


def add_pair(earlier, later):
    return (earlier[0] + later[0], earlier[1] + later[1])


def local(queries, keys, values, gain, ridge, prior_gram, prior_cross, cotangent):
    highest = lax.Precision.HIGHEST
    row_count, width = queries.shape
    heads_here = width // DH

    def split_heads(array):
        return array.reshape(row_count, heads_here, DH).transpose(1, 0, 2)

    def join_heads(array):
        return array.transpose(1, 0, 2).reshape(row_count, width)

    head_q = split_heads(queries)
    head_k = split_heads(keys)
    head_v = split_heads(values)
    own_gram = jnp.einsum("hti,htj->hij", head_k, head_k, precision=highest)
    own_cross = jnp.einsum("hti,htj->hij", head_k, head_v, precision=highest)
    position = lax.axis_index("seq")
    first_row = position * row_count
    empty = jnp.zeros_like(own_gram)
    lower_gram, lower_cross = prefix((own_gram, own_cross), "seq", add_pair, (empty, empty), False)
    start_gram = prior_gram + lower_gram
    start_cross = prior_cross + lower_cross
    batched = jax.vmap(jax.checkpoint(block_forward), in_axes=(0, 0, 0, 0, 0, 0, None))

    def local_forward(first, second, third, fourth, fifth):
        return batched(first, second, third, fourth, fifth, ridge, first_row)

    outputs, pullback = jax.vjp(local_forward, head_q, head_k, head_v, start_gram, start_cross)
    mixed = join_heads(outputs)
    scaled_cot = gain * cotangent
    local_square = jnp.sum(mixed * mixed, axis=1)
    local_cross = jnp.sum(scaled_cot * mixed, axis=1)
    total_square = lax.psum(local_square, "head")
    feature_count = width * lax.axis_size("head")
    inverse = lax.rsqrt(total_square / feature_count + epsilon)[:, None]
    normed = mixed * inverse * gain
    total_cross = lax.psum(local_cross, "head")
    grad_mixed = (
        inverse * scaled_cot
        - mixed * (inverse * inverse * inverse) * (total_cross / feature_count)[:, None]
    )
    grad_q, grad_k, grad_v, grad_gram, grad_cross = pullback(split_heads(grad_mixed))
    later_gram, later_cross = prefix((grad_gram, grad_cross), "seq", add_pair, (empty, empty), True)
    symmetric = later_gram + jnp.transpose(later_gram, (0, 2, 1))
    grad_k = (
        grad_k
        + jnp.einsum("hti,hij->htj", head_k, symmetric, precision=highest)
        + jnp.einsum("htj,hij->hti", head_v, later_cross, precision=highest)
    )
    grad_v = grad_v + jnp.einsum("hti,hij->htj", head_k, later_cross, precision=highest)
    return (normed, join_heads(grad_q), join_heads(grad_k), join_heads(grad_v))


def solution(mesh):
    in_specs = (
        P("seq", "head"),
        P("seq", "head"),
        P("seq", "head"),
        P("head"),
        P("head"),
        P("head", None, None),
        P("head", None, None),
        P("seq", "head"),
    )
    out_specs = (P("seq", "head"), P("seq", "head"), P("seq", "head"), P("seq", "head"))
    return jax.shard_map(local, mesh=mesh, in_specs=in_specs, out_specs=out_specs, check_vma=False)
```

profile of v0, /device:TPU:1, one launch (start us, length us, event | category | flops | bytes accessed | tf_op | source)
XLA Modules:
  0.0 445.6 jit_solution(2497507912870803327)
XLA Ops:
  7.2 2.3 fusion.85
  9.7 2.2 fusion.86
  11.9 1.1 copy.57
  13.2 1.1 copy.58
  14.7 49.3 %all-gather.9.cloned.1.call-done = f32[4096,128]{1,0:T(8,128)} async-done(((f32[128,128]{1,0:T(8,128)}), f32[4096,128]{1,0:T(8,128)}) %all-gather.9.cloned.1.call-update) | async-done | bytes 2097168 | tf_op jit(solution)/shard_map/all_gather | solution.py:15
  63.9 51.1 %all-gather.11.cloned.1.call-done = f32[4096,128]{1,0:T(8,128)} async-done(((f32[128,128]{1,0:T(8,128)}), f32[4096,128]{1,0:T(8,128)}) %all-gather.11.cloned.1.call-update) | async-done | bytes 2097168 | tf_op jit(solution)/shard_map/all_gather | solution.py:15
  116.9 30.1 %while.107 = (s32[]{:T(128)}, f32[1,512,128]{1,2,0:T(8,128)S(1)}, f32[1,512,128]{1,2,0:T(8,128)S(1)}, f32[1,512,128]{1,2,0:T(8,128)S(1)}, f32[1,512,1]{1,2,0:T(1...) while((s32[]{:T(128)}, f32[1,512,128]{1,2,0:T(8,128)S(1)}, ...), condition=%wide.region_6.7_spmd.clone, body=%wide.region_3.6_spmd.clone.sunk | while | flops 907675648 | bytes 6125703 | solution.py:54
  117.9 1.2 fusion.135
  121.7 1.2 fusion.135
  125.5 1.2 fusion.135
  129.2 1.2 fusion.135
  133.0 1.2 fusion.135
  136.8 1.2 fusion.135
  140.5 1.2 fusion.135
  144.3 1.2 fusion.135
  148.1 1.2 fusion.87
  149.8 13.8 %all-reduce = (f32[512]{0:T(512)S(1)}, f32[512]{0:T(512)S(1)}) all-reduce(f32[512]{0:T(512)S(1)} %get-tuple-element.1178, f32[512]{0:T(512)S(1)} %get-tuple-element.1177), channel_id=1, replica_groups=mesh['seq'=32,'head'=8] {'head'}, use_global_device_ids=true, to_apply=%region_8.9 | all-reduce | flops 1024 | bytes 8192 | tf_op jit(solution)/shard_map/psum | solution.py:97
  164.9 63.0 %while.108 = (s32[]{:T(128)}, f32[1,512,128]{1,2,0:T(8,128)S(1)}, f32[1,512,128]{1,2,0:T(8,128)S(1)}, f32[1,512,128]{1,2,0:T(8,128)S(1)}, f32[1,512,1]{1,2,0:T(1...) while((s32[]{:T(128)}, f32[1,512,128]{1,2,0:T(8,128)S(1)}, ...), condition=%wide.region_15.16_spmd.clone, body=%wide.region_12.15_spmd.clone.sunk | while | flops 907677696 | bytes 8506591 | solution.py:54
  164.9 2.0 bitcast_dynamic-update-slice_fusion.6
  166.9 1.2 fusion.138
  172.8 2.0 bitcast_dynamic-update-slice_fusion.6
  174.8 1.2 fusion.138
  180.7 2.0 bitcast_dynamic-update-slice_fusion.6
  182.6 1.2 fusion.138
  188.5 2.0 bitcast_dynamic-update-slice_fusion.6
  190.6 1.2 fusion.138
  196.4 2.0 bitcast_dynamic-update-slice_fusion.6
  198.4 1.2 fusion.138
  204.2 2.0 bitcast_dynamic-update-slice_fusion.6
  206.2 1.2 fusion.138
  212.1 2.0 bitcast_dynamic-update-slice_fusion.6
  214.1 1.2 fusion.138
  219.9 2.0 bitcast_dynamic-update-slice_fusion.6
  222.0 1.2 fusion.138
  232.8 99.0 %while.109 = (s32[]{:T(128)}, f32[1,512,128]{1,2,0:T(8,128)S(1)}, f32[1,128,128]{1,2,0:T(8,128)S(1)}, f32[1,512,128]{2,1,0:T(8,128)S(1)}, f32[1,512,128]{2,1,0:T...) while((s32[]{:T(128)}, f32[1,512,128]{1,2,0:T(8,128)S(1)}, ...), condition=%wide.region_20.21_spmd.clone, body=%wide.region_16.20_spmd.clone.sunk | while | flops 1814796800 | bytes 15208740 | solution.py:54
  241.9 2.0 fusion.155
  254.2 2.0 fusion.155
  266.6 2.0 fusion.155
  278.9 2.0 fusion.155
  291.3 2.0 fusion.155
  294.6 1.1 constant_dynamic-slice_fusion.15
  303.7 2.0 fusion.155
  316.1 2.0 fusion.155
  328.5 2.0 fusion.155
  332.7 1.8 copy.75
  337.1 1.8 fusion.64
  339.0 69.1 %all-gather.13.cloned.1.call-done = f32[32,128,128]{2,1,0:T(8,128)} async-done(((f32[1,128,128]{2,1,0:T(8,128)}), f32[32,128,128]{2,1,0:T(8,128)}) %all-gather.13.cloned.1.call-update) | async-done | bytes 2097168 | tf_op jit(solution)/shard_map/all_gather | solution.py:15
  408.1 28.2 %while.106 = (s32[]{:T(128)}, f32[1,128,128]{2,1,0:T(8,128)S(1)}, f32[1,128,128]{2,1,0:T(8,128)S(1)}, s32[]{:T(128)}, f32[32,1,128,128]{3,2,1,0:T(8,128)}, /*ind...) while((s32[]{:T(128)}, f32[1,128,128]{2,1,0:T(8,128)S(1)}, ...), condition=%wide.region_22.23_spmd, body=%wide.region_21.22_spmd.sunk | while | flops 32774 | bytes 393367 | solution.py:24
  (410 shorter events, 182.2 us)
Async XLA Ops:
  7.2 2.5 copy-start
  7.2 7.3 %copy-start.4 = (f32[512,128]{1,0:T(8,128)S(1)}, f32[512,128]{1,0:T(8,128)}, u32[]{:S(2)}) copy-start(f32[512,128]{1,0:T(8,128)} %param.18) | copy-start | bytes 786436
  7.2 7.2 %copy-start.8 = (f32[512,128]{1,0:T(8,128)S(1)}, f32[512,128]{1,0:T(8,128)}, u32[]{:S(2)}) copy-start(f32[512,128]{1,0:T(8,128)} %param.25) | copy-start | bytes 786436
  7.2 56.7 %all-gather.9.cloned.1.call-start = ((), (), s32[]{:S(2)}) async-start(), calls=%async_computation | async-start | bytes 2162688 | tf_op jit(solution)/shard_map/all_gather | solution.py:15
  9.6 105.5 %all-gather.11.cloned.1.call-start = ((), (), s32[]{:S(2)}) async-start(), calls=%async_computation.1 | async-start | bytes 2162688 | tf_op jit(solution)/shard_map/all_gather | solution.py:15
  11.9 327.1 %all-gather.15.cloned.1.call-start = ((), (), s32[]{:S(2)}) async-start(), calls=%async_computation.3 | async-start | bytes 2162688 | tf_op jit(solution)/shard_map/all_gather | solution.py:15
  13.2 103.7 %copy-start.1 = (f32[512,128]{1,0:T(8,128)S(1)}, f32[512,128]{1,0:T(8,128)}, u32[]{:S(2)}) copy-start(f32[512,128]{1,0:T(8,128)} %param.19) | copy-start | bytes 786436
  147.0 2.3 copy-start.10
  147.0 2.3 copy-start.11
  164.4 67.8 %copy-start.6 = (f32[1,512,128]{1,2,0:T(8,128)}, f32[1,512,128]{1,2,0:T(8,128)S(1)}, u32[]{:S(2)}) copy-start(f32[1,512,128]{1,2,0:T(8,128)S(1)} %get-tuple-element.759) | copy-start | bytes 786436
  228.2 4.6 %copy-start.9 = (f32[1,512,1]{1,2,0:T(1,128)S(1)}, f32[1,512,1]{1,2,0:T(1,128)}, u32[]{:S(2)}) copy-start(f32[1,512,1]{1,2,0:T(1,128)} %custom-call.6) | copy-start | bytes 6148
  229.0 179.1 %all-gather.13.cloned.1.call-start = ((), (), s32[]{:S(2)}) async-start(), calls=%async_computation.2 | async-start | bytes 2162688 | tf_op jit(solution)/shard_map/all_gather | solution.py:15
  230.2 1.0 copy-start.2
  331.8 3.7 copy-start.7
  332.6 3.7 copy-start.5
  334.5 2.6 copy-start.3
Sparse Core Ops, SparseCore 0:
  11.1 52.7 all-gather.8
  67.1 47.9 all-gather.10
  229.1 75.3 all-gather.14
  332.7 75.3 all-gather.12
where the time goes:
time: 449 us; the launch traced here: 446 us
  waiting for transfers between devices  170 us (38%)
  matrix products  112 us (25%)
  other arithmetic  89.9 us (20%)
  local copies, waits for them, and re-layouts  42.8 us (10%)
  between operations  14.3 us (3%)
  blocking collectives  13.8 us (3%)
    all_gather x4, waiting for transfers between devices, prefix(): gathered = jax.tree.map(lambda a: lax.all_gather(a, axis), part)  169 us
    dot_general x32, matrix products, apply_system(): jnp.dot(inner, keyset, precision=highest)  43.5 us
    dot_general x32, matrix products, apply_system(): inner = jnp.dot(search, keyset.T, precision=highest) * causal  38 us
    dynamic_slice x56, local copies, waits for them, and re-layouts, block_forward(): (solution, _, _, _), _ = lax.scan(cg_step, start, None, length=ITERS)  30.2 us
    add x31, other arithmetic, add_pair(): return (earlier[0] + later[0], earlier[1] + later[1])  28.2 us
    dynamic_update_slice x32, other arithmetic, block_forward(): (solution, _, _, _), _ = lax.scan(cg_step, start, None, length=ITERS)  21.7 us
    mul x24, other arithmetic, block_forward(): ridge_value * (first_row + places + 1).astype(jnp.float32)[:, None]  15.7 us
    dot_general x32, matrix products, apply_system(): jnp.dot(search, start_gram, precision=highest)  15.3 us
  transfers between devices with their start and end apart: 4, of which 3 were waited for; matrix products, arithmetic and copies ran while one was open for 25% of the time, Pallas kernels for 0%

commit v1 on v0

--- a/solution.py
+++ b/solution.py
@@ -94,7 +94,7 @@
     scaled_cot = gain * cotangent
     local_square = jnp.sum(mixed * mixed, axis=1)
     local_cross = jnp.sum(scaled_cot * mixed, axis=1)
-    total_square = lax.psum(local_square, "head")
+    total_square = jnp.sum(lax.all_gather(local_square, "head"), axis=0)
     feature_count = width * lax.axis_size("head")
     inverse = lax.rsqrt(total_square / feature_count + epsilon)[:, None]
     normed = mixed * inverse * gain

time: 449 us -> 470 us (1.047)
  blocking collectives: 13.8 us -> 29.2 us
  waiting for transfers between devices: 170 us -> 175 us
    all_gather x0 -> x1, blocking collectives: none -> 18.4 us  [local(): total_square = jnp.sum(lax.all_gather(local_square, 'head'), axis=0)]
    all_gather x4, waiting for transfers between devices: 169 us -> 175 us  [prefix(): gathered = jax.tree.map(lambda a: lax.all_gather(a, axis), part)]
  transfers between devices with their start and end apart: 4 -> 4, of which waited for: 3 -> 3; matrix products, arithmetic and copies ran while one was open for 25% -> 24% of each run, Pallas kernels for 0% -> 0%
where the time goes in v1:
time: 470 us; the launch traced here: 467 us
  waiting for transfers between devices  175 us (37%)
  matrix products  112 us (24%)
  other arithmetic  89.9 us (19%)
  local copies, waits for them, and re-layouts  42.9 us (9%)
  blocking collectives  29.2 us (6%)
  between operations  14.3 us (3%)
    all_gather x4, waiting for transfers between devices, prefix(): gathered = jax.tree.map(lambda a: lax.all_gather(a, axis), part)  175 us
    dot_general x32, matrix products, apply_system(): jnp.dot(inner, keyset, precision=highest)  43.5 us
    dot_general x32, matrix products, apply_system(): inner = jnp.dot(search, keyset.T, precision=highest) * causal  38 us
    dynamic_slice x56, local copies, waits for them, and re-layouts, block_forward(): (solution, _, _, _), _ = lax.scan(cg_step, start, None, length=ITERS)  30.1 us
    add x31, other arithmetic, add_pair(): return (earlier[0] + later[0], earlier[1] + later[1])  28.2 us
    dynamic_update_slice x32, other arithmetic, block_forward(): (solution, _, _, _), _ = lax.scan(cg_step, start, None, length=ITERS)  21.7 us
    all_gather x1, blocking collectives, local(): total_square = jnp.sum(lax.all_gather(local_square, 'head'), axis=0)  18.4 us
    mul x24, other arithmetic, block_forward(): ridge_value * (first_row + places + 1).astype(jnp.float32)[:, None]  15.7 us
  transfers between devices with their start and end apart: 4, of which 3 were waited for; matrix products, arithmetic and copies ran while one was open for 24% of the time, Pallas kernels for 0%

profile of v1, /device:TPU:1, one launch (start us, length us, event | category | flops | bytes accessed | tf_op | source)
XLA Modules:
  0.0 466.7 jit_solution(14232697312443214898)
XLA Ops:
  7.2 2.3 fusion.85
  9.7 2.2 fusion.86
  11.9 1.1 copy.57
  13.2 1.1 copy.58
  14.7 49.3 %all-gather.11.cloned.1.call-done = f32[4096,128]{1,0:T(8,128)} async-done(((f32[128,128]{1,0:T(8,128)}), f32[4096,128]{1,0:T(8,128)}) %all-gather.11.cloned.1.call-update) | async-done | bytes 2097168 | tf_op jit(solution)/shard_map/all_gather | solution.py:15
  63.9 51.1 %all-gather.13.cloned.1.call-done = f32[4096,128]{1,0:T(8,128)} async-done(((f32[128,128]{1,0:T(8,128)}), f32[4096,128]{1,0:T(8,128)}) %all-gather.13.cloned.1.call-update) | async-done | bytes 2097168 | tf_op jit(solution)/shard_map/all_gather | solution.py:15
  116.9 30.1 %while.107 = (s32[]{:T(128)}, f32[1,512,128]{1,2,0:T(8,128)S(1)}, f32[1,512,128]{1,2,0:T(8,128)S(1)}, f32[1,512,128]{1,2,0:T(8,128)S(1)}, f32[1,512,1]{1,2,0:T(1...) while((s32[]{:T(128)}, f32[1,512,128]{1,2,0:T(8,128)S(1)}, ...), condition=%wide.region_6.7_spmd.clone, body=%wide.region_3.6_spmd.clone.sunk | while | flops 907675648 | bytes 6125703 | solution.py:54
  117.9 1.2 fusion.135
  121.7 1.2 fusion.135
  125.5 1.2 fusion.135
  129.2 1.2 fusion.135
  133.0 1.2 fusion.135
  136.8 1.2 fusion.135
  140.5 1.2 fusion.135
  144.3 1.2 fusion.135
  148.1 1.2 fusion.87
  149.8 18.4 %all-gather.5 = f32[8,1,512]{2,1,0:T(1,128)S(1)} all-gather(f32[1,1,512]{2,1,0:T(1,128)S(1)} %bitcast.515), channel_id=4, replica_groups=mesh['seq'=32,'head'=8] {'head'}, dimensions={0}, use_global_device_ids=true | all-gather | bytes 18432 | tf_op jit(solution)/shard_map/all_gather | solution.py:97
  168.2 10.9 %psum.7 = f32[512]{0:T(512)S(1)} all-reduce(f32[512]{0:T(512)S(1)} %get-tuple-element.1177), channel_id=1, replica_groups=mesh['seq'=32,'head'=8] {'head'}, use_global_device_ids=true, to_apply=%region_10.11 | all-reduce | flops 512 | bytes 4096 | tf_op jit(solution)/shard_map/psum | solution.py:101
  180.3 63.0 %while.108 = (s32[]{:T(128)}, f32[1,512,128]{1,2,0:T(8,128)S(1)}, f32[1,512,128]{1,2,0:T(8,128)S(1)}, f32[1,512,128]{1,2,0:T(8,128)S(1)}, f32[1,512,1]{1,2,0:T(1...) while((s32[]{:T(128)}, f32[1,512,128]{1,2,0:T(8,128)S(1)}, ...), condition=%wide.region_15.16_spmd.clone, body=%wide.region_12.15_spmd.clone.sunk | while | flops 907677696 | bytes 8506591 | solution.py:54
  180.4 2.0 bitcast_dynamic-update-slice_fusion.6
  182.4 1.2 fusion.138
  188.2 2.0 bitcast_dynamic-update-slice_fusion.6
  190.3 1.2 fusion.138
  196.1 2.0 bitcast_dynamic-update-slice_fusion.6
  198.1 1.2 fusion.138
  204.0 2.0 bitcast_dynamic-update-slice_fusion.6
  206.0 1.2 fusion.138
  211.9 2.0 bitcast_dynamic-update-slice_fusion.6
  213.9 1.2 fusion.138
  219.7 2.0 bitcast_dynamic-update-slice_fusion.6
  221.7 1.2 fusion.138
  227.6 2.0 bitcast_dynamic-update-slice_fusion.6
  229.6 1.2 fusion.138
  235.4 2.0 bitcast_dynamic-update-slice_fusion.6
  237.5 1.2 fusion.138
  248.4 98.9 %while.109 = (s32[]{:T(128)}, f32[1,512,128]{1,2,0:T(8,128)S(1)}, f32[1,128,128]{1,2,0:T(8,128)S(1)}, f32[1,512,128]{2,1,0:T(8,128)S(1)}, f32[1,512,128]{2,1,0:T...) while((s32[]{:T(128)}, f32[1,512,128]{1,2,0:T(8,128)S(1)}, ...), condition=%wide.region_20.21_spmd.clone, body=%wide.region_16.20_spmd.clone.sunk | while | flops 1814796800 | bytes 15208740 | solution.py:54
  257.4 2.0 fusion.155
  269.8 2.0 fusion.155
  282.1 2.0 fusion.155
  294.5 2.0 fusion.155
  306.8 2.0 fusion.155
  319.2 2.0 fusion.155
  331.6 2.0 fusion.155
  343.9 2.0 fusion.155
  348.2 1.8 copy.75
  352.6 1.8 fusion.64
  354.5 74.7 %all-gather.15.cloned.1.call-done = f32[32,128,128]{2,1,0:T(8,128)} async-done(((f32[1,128,128]{2,1,0:T(8,128)}), f32[32,128,128]{2,1,0:T(8,128)}) %all-gather.15.cloned.1.call-update) | async-done | bytes 2097168 | tf_op jit(solution)/shard_map/all_gather | solution.py:15
  429.2 28.2 %while.106 = (s32[]{:T(128)}, f32[1,128,128]{2,1,0:T(8,128)S(1)}, f32[1,128,128]{2,1,0:T(8,128)S(1)}, s32[]{:T(128)}, f32[32,1,128,128]{3,2,1,0:T(8,128)}, /*ind...) while((s32[]{:T(128)}, f32[1,128,128]{2,1,0:T(8,128)S(1)}, ...), condition=%wide.region_22.23_spmd, body=%wide.region_21.22_spmd.sunk | while | flops 32774 | bytes 393367 | solution.py:24
  (413 shorter events, 183.3 us)
Async XLA Ops:
  7.2 2.5 copy-start
  7.2 7.3 %copy-start.4 = (f32[512,128]{1,0:T(8,128)S(1)}, f32[512,128]{1,0:T(8,128)}, u32[]{:S(2)}) copy-start(f32[512,128]{1,0:T(8,128)} %param.18) | copy-start | bytes 786436
  7.2 7.2 %copy-start.8 = (f32[512,128]{1,0:T(8,128)S(1)}, f32[512,128]{1,0:T(8,128)}, u32[]{:S(2)}) copy-start(f32[512,128]{1,0:T(8,128)} %param.25) | copy-start | bytes 786436
  7.2 56.7 %all-gather.11.cloned.1.call-start = ((), (), s32[]{:S(2)}) async-start(), calls=%async_computation | async-start | bytes 2162688 | tf_op jit(solution)/shard_map/all_gather | solution.py:15
  9.6 105.5 %all-gather.13.cloned.1.call-start = ((), (), s32[]{:S(2)}) async-start(), calls=%async_computation.1 | async-start | bytes 2162688 | tf_op jit(solution)/shard_map/all_gather | solution.py:15
  11.9 342.6 %all-gather.17.cloned.1.call-start = ((), (), s32[]{:S(2)}) async-start(), calls=%async_computation.3 | async-start | bytes 2162688 | tf_op jit(solution)/shard_map/all_gather | solution.py:15
  13.2 103.7 %copy-start.1 = (f32[512,128]{1,0:T(8,128)S(1)}, f32[512,128]{1,0:T(8,128)}, u32[]{:S(2)}) copy-start(f32[512,128]{1,0:T(8,128)} %param.19) | copy-start | bytes 786436
  147.0 2.3 copy-start.10
  147.0 2.3 copy-start.11
  179.9 67.9 %copy-start.6 = (f32[1,512,128]{1,2,0:T(8,128)}, f32[1,512,128]{1,2,0:T(8,128)S(1)}, u32[]{:S(2)}) copy-start(f32[1,512,128]{1,2,0:T(8,128)S(1)} %get-tuple-element.759) | copy-start | bytes 786436
  243.8 4.6 copy-start.9
  244.5 184.7 %all-gather.15.cloned.1.call-start = ((), (), s32[]{:S(2)}) async-start(), calls=%async_computation.2 | async-start | bytes 2162688 | tf_op jit(solution)/shard_map/all_gather | solution.py:15
  245.8 1.0 copy-start.2
  347.3 3.7 copy-start.7
  348.1 3.7 copy-start.5
  350.0 2.6 copy-start.3
Sparse Core Ops, SparseCore 0:
  11.1 52.7 all-gather.10
  67.1 47.9 all-gather.12
  244.6 80.9 all-gather.16
  348.2 80.9 all-gather.14
